TPU v7x, 512 devices: a whole 4x4x16 slice. The times are simulated.
512 devices in a mesh: section: 16 (over x, z_hi, core), dp: 32 (over y, z_lo).
Axes of the slice: x: 4, y: 4, z: 16 (z_hi: 2, z_lo: 8; z = z_hi * 8 + z_lo), core: 2. Of those that a mesh axis runs over, the one named last changes fastest.
Arguments:
- arriving_activations: bfloat16 [16, 64, 12, 12, 256], P('section', 'dp'), may hold values from -6 to 6
- fresh_images: bfloat16 [3, 64, 12, 12, 256], P(None, 'dp'), may hold values from -6 to 6
- saved_inputs: bfloat16 [4, 16, 64, 12, 12, 256], P(None, 'section', 'dp'), may hold values from -6 to 6
- arriving_gradients: bfloat16 [16, 64, 12, 12, 256], P('section', 'dp'), may hold values from -6 to 6
- fresh_gradients: bfloat16 [3, 64, 12, 12, 256], P(None, 'dp'), may hold values from -6 to 6
- feed_order: int32 [3], replicated, may hold values from 0 to 2, each once
- forward_weight: bfloat16 [16, 2304, 256], P('section'), may hold values from -0.125 to 0.125
- forward_gain: float32 [16, 256], P('section'), may hold values from 0.1 to 1.9
- forward_bias: float32 [16, 256], P('section'), may hold values from -3 to 3
- backward_weight: bfloat16 [16, 2304, 256], P('section'), may hold values from -0.125 to 0.125
- backward_gain: float32 [16, 256], P('section'), may hold values from 0.1 to 1.9
- backward_bias: float32 [16, 256], P('section'), may hold values from -3 to 3
Outputs:
- section_outputs: float32 [4, 16, 64, 12, 12, 256], P(None, 'section', 'dp')
- input_gradients: float32 [4, 16, 64, 12, 12, 256], P(None, 'section', 'dp')
- weight_gradient: float32 [16, 2304, 256], P('section', 'dp')
Inputs may be any that keep to these rules, and one draw needn't show every extreme that they name: `feed_order`: each of 0 to 2 appears once.
All inputs are finite; a program needn't handle non-finite values.
Results may differ from a plain program's by a relative error of at most 0.0044.
Values sent between devices are 32-bit elements; how exact they have to be, the bound alone decides.
A program may use at most 64 MiB of HBM per device.

v0:
```python
import jax
import jax.numpy as jnp
from jax import lax
from jax.sharding import PartitionSpec as P

GROUPS = 32
TICKS = 4


def passed_along(block, axis, distance):
    devices = range(lax.axis_size(axis))
    route = [(i - distance, i) for i in devices if i - distance in devices]
    return lax.ppermute(block, axis, route)


def group_norm_silu(values, gain, bias):
    grouped = values.reshape(values.shape[0], values.shape[1] * values.shape[2], GROUPS, -1)
    average = jnp.mean(grouped, axis=(1, 3), keepdims=True)
    spread = jnp.mean(jnp.square(grouped - average), axis=(1, 3), keepdims=True)
    normed = ((grouped - average) * lax.rsqrt(spread + 1e-05)).reshape(values.shape)
    scaled = normed * gain + bias
    return scaled * jax.nn.sigmoid(scaled)


def patches(images):
    rows = images.shape[1]
    cols = images.shape[2]
    padded = jnp.pad(images, ((0, 0), (1, 1), (1, 1), (0, 0)))
    shifted = [
        padded[:, shift_row : shift_row + rows, shift_col : shift_col + cols, :]
        for shift_row in range(3)
        for shift_col in range(3)
    ]
    return jnp.concatenate(shifted, axis=-1).reshape(-1, 9 * images.shape[3])


def flipped(weight):
    channels = weight.shape[1]
    return (
        weight.reshape(3, 3, channels, channels)[::-1, ::-1]
        .transpose(0, 1, 3, 2)
        .reshape(9 * channels, channels)
    )


def forward_layer(widened, weight, gain, bias):
    hidden = group_norm_silu(widened, gain, bias).astype(jnp.bfloat16)
    convolved = jnp.dot(patches(hidden), weight, preferred_element_type=jnp.float32).reshape(
        widened.shape
    )
    return widened + convolved


def backward_layer(saved, incoming, narrow, weight, gain, bias):
    widened = saved.astype(jnp.float32)
    activated, pullback = jax.vjp(lambda values: group_norm_silu(values, gain, bias), widened)
    hidden = activated.astype(jnp.bfloat16)
    hidden_grad = jnp.dot(
        patches(narrow), flipped(weight), preferred_element_type=jnp.float32
    ).reshape(saved.shape)
    (through_norm,) = pullback(hidden_grad)
    return (incoming + through_norm, patches(hidden))


def shards(
    arriving_activations,
    fresh_images,
    saved_inputs,
    arriving_gradients,
    fresh_gradients,
    feed_order,
    forward_weight,
    forward_gain,
    forward_bias,
    backward_weight,
    backward_gain,
    backward_bias,
):
    section_pos = lax.axis_index("section")
    act_in = arriving_activations[0].astype(jnp.float32)
    grad_in = arriving_gradients[0].astype(jnp.float32)
    act_out = act_in
    grad_out = grad_in
    emitted = []
    returned = []
    column_list = []
    incoming_list = []
    for tick_num in range(TICKS):
        if tick_num > 0:
            index = feed_order[tick_num - 1]
            arrived, arrived_grad = passed_along((act_out, grad_out), "section", 1)
            chosen = lax.dynamic_index_in_dim(fresh_images, index, 0, keepdims=False).astype(
                jnp.float32
            )
            act_in = jnp.where(section_pos == 0, chosen, arrived)
            chosen_grad = lax.dynamic_index_in_dim(
                fresh_gradients, index, 0, keepdims=False
            ).astype(jnp.float32)
            grad_in = jnp.where(section_pos == 0, chosen_grad, arrived_grad)
        narrow = grad_in.astype(jnp.bfloat16)
        act_out = forward_layer(act_in, forward_weight[0], forward_gain[0], forward_bias[0])
        grad_out, columns = backward_layer(
            saved_inputs[tick_num, 0],
            grad_in,
            narrow,
            backward_weight[0],
            backward_gain[0],
            backward_bias[0],
        )
        emitted.append(act_out)
        returned.append(grad_out)
        column_list.append(columns)
        incoming_list.append(narrow.reshape(-1, narrow.shape[3]))
    column_rows = jnp.concatenate(column_list, axis=0)
    incoming_rows = jnp.concatenate(incoming_list, axis=0)
    factor = 1.0 / (lax.axis_size("dp") * act_in.shape[0])
    total = (
        lax.dot_general(
            column_rows, incoming_rows, (((0,), (0,)), ((), ())), preferred_element_type=jnp.float32
        )
        * factor
    )
    shard_sum = lax.psum_scatter(total, "dp", scatter_dimension=0, tiled=True)
    return (jnp.stack(emitted)[:, None], jnp.stack(returned)[:, None], shard_sum[None])


def solution(mesh):
    placed = (
        P("section", "dp", None, None, None),
        P(None, "dp", None, None, None),
        P(None, "section", "dp", None, None, None),
        P("section", "dp", None, None, None),
        P(None, "dp", None, None, None),
        P(),
        P("section", None, None),
        P("section", None),
        P("section", None),
        P("section", None, None),
        P("section", None),
        P("section", None),
    )
    return jax.shard_map(
        shards,
        mesh=mesh,
        in_specs=placed,
        out_specs=(
            P(None, "section", "dp", None, None, None),
            P(None, "section", "dp", None, None, None),
            P("section", "dp", None),
        ),
        check_vma=False,
    )
```

profile of v0, /device:TPU:4, one launch (start us, length us, event | category | flops | bytes accessed | tf_op | source)
XLA Modules:
  0.0 453.9 jit_solution(5519394117406257145)
XLA Ops:
  16.3 1.3 reverse_bitcast_fusion
  17.7 1.5 copy.35
  19.3 2.6 multiply_reduce_fusion.6
  23.2 1.9 collective-permute-start.3
  26.8 1.4 convolution_add_fusion.3
  28.2 15.9 %collective-permute-start = (f32[2,12,12,256]{3,2,1,0:T(8,128)}, f32[2,12,12,256]{3,2,1,0:T(8,128)S(1)}, u32[]{:S(2)}, u32[]{:S(2)}) collective-permute-start(f32[2,12,12,256]{3,2,1,0:T(8,128)} %convolution_add_fusion.3), channel_id=1, source_target_pairs={{0,32},{32,64},{64,96},{96,128},{128,160},{160,192},{192,224},{224... | collective-permute-start | bytes 884744 | tf_op jit(solution)/shard_map/ppermute | solution.py:13
  58.8 2.1 constant_dynamic-slice_fusion
  60.8 1.4 constant_dynamic-slice_fusion.3
  70.7 2.2 multiply_reduce_fusion.5
  74.6 2.0 fusion.92
  76.6 1.9 collective-permute-start.4
  82.2 2.1 collective-permute-start.1
  86.5 16.8 %collective-permute-done.4 = f32[2,12,12,256]{3,2,1,0:T(8,128)} collective-permute-done((f32[2,12,12,256]{3,2,1,0:T(8,128)}, f32[2,12,12,256]{3,2,1,0:T(8,128)}, u32[]{:S(2)}, u32[]{:S(2)}) %collective-permute-start.4) | collective-permute-done | bytes 294944 | tf_op jit(solution)/shard_map/ppermute | solution.py:13
  111.8 3.0 multiply_reduce_fusion.4
  115.8 2.1 fusion.109
  117.9 1.9 collective-permute-start.5
  120.6 4.1 collective-permute-done.1
  128.0 17.2 %collective-permute-done.5 = f32[2,12,12,256]{3,2,1,0:T(8,128)} collective-permute-done((f32[2,12,12,256]{3,2,1,0:T(8,128)}, f32[2,12,12,256]{3,2,1,0:T(8,128)}, u32[]{:S(2)}, u32[]{:S(2)}) %collective-permute-start.5) | collective-permute-done | bytes 294944 | tf_op jit(solution)/shard_map/ppermute | solution.py:13
  153.2 3.0 multiply_reduce_fusion.3
  157.8 2.1 fusion.126
  160.2 2.1 constant_dynamic-update-slice_fusion.76
  166.7 3.2 reshape.405
  172.2 3.2 reshape.406
  178.5 3.2 reshape.407
  183.9 3.2 reshape.408
  187.1 4.7 %fusion.8 = f32[2304,256]{1,0:T(8,128)} fusion(bf16[288,2304]{1,0:T(8,128)(2,1)} %reshape.408, bf16[288,2304]{1,0:T(8,128)(2,1)} %reshape.407, bf16[288,2304]{1,0:T(8,128)(2,1)} %reshape.406, bf16[288,2304]{1,0:T(8,128)(2,1)} %reshape.405, bf16[288,256]{1,0:T(8,128)(2,1)S(1)} %reshape.412, bf16[288,256]{1,0:T(8,128)(2,1)S(1)} %copy-done.18, ...), kind=kOutput, calls=%fused_computation.8 | convolution fusion | flops 1383137280 | bytes 8257536 | tf_op jit(solution)/shard_map/dot_general | solution.py:118
  194.3 2.1 collective-permute-start.2
  196.5 1.3 maximum_bitcast_fusion.1
  197.8 2.0 copy.45
  199.8 19.7 %collective-permute-done.2 = f32[2,12,12,256]{3,2,1,0:T(8,128)S(1)} collective-permute-done((f32[2,12,12,256]{3,2,1,0:T(8,128)S(1)}, f32[2,12,12,256]{3,2,1,0:T(8,128)S(1)}, u32[]{:S(2)}, u32[]{:S(2)}) %collective-permute-start.2) | collective-permute-done | bytes 294944 | tf_op jit(solution)/shard_map/ppermute | solution.py:13
  223.2 2.0 copy.44
  225.2 221.9 %reduce-scatter.2.cloned.1.call-done = f32[72,256]{1,0:T(8,128)} async-done(((f32[2304,256]{1,0:T(8,128)}), f32[72,256]{1,0:T(8,128)}) %reduce-scatter.2.cloned.1.call-update) | async-done | bytes 73744 | tf_op jit(solution)/shard_map/reduce_scatter | solution.py:123
  (363 shorter events, 77.5 us)
Async XLA Ops:
  7.2 19.6 %copy-start = (bf16[1,2304,256]{2,1,0:T(8,128)(2,1)S(1)}, bf16[1,2304,256]{2,1,0:T(8,128)(2,1)}, u32[]{:S(2)}) copy-start(bf16[1,2304,256]{2,1,0:T(8,128)(2,1)} %param.18) | copy-start | bytes 3538948
  7.2 4.2 copy-start.8
  7.2 439.9 %reduce-scatter.2.cloned.1.call-start = ((), (), s32[]{:S(2)}) async-start(), calls=%async_computation.1 | async-start | bytes 2433024 | tf_op jit(solution)/shard_map/reduce_scatter | solution.py:123
  8.3 6.8 %copy-start.15 = (bf16[4,1,2,12,12,256]{5,2,4,3,1,0:T(2,128)(2,1)S(1)}, bf16[4,1,2,12,12,256]{5,2,4,3,1,0:T(2,128)(2,1)}, u32[]{:S(2)}) copy-start(bf16[4,1,2,12,12,256]{5,2,4,3,1,0:T(2,128)(2,1)} %param.14) | copy-start | bytes 1769476
  16.3 6.6 %copy-start.31 = (f32[2,256]{1,0:T(2,128)}, f32[2,256]{1,0:T(2,128)S(1)}, u32[]{:S(2)}) copy-start(f32[2,256]{1,0:T(2,128)S(1)} %mul.459) | copy-start | bytes 6148
  21.9 4.1 copy-start.19
  21.9 4.1 copy-start.21
  23.2 39.0 %collective-permute-start.3 = (f32[2,12,12,256]{3,2,1,0:T(8,128)S(1)}, f32[2,12,12,256]{3,2,1,0:T(8,128)}, u32[]{:S(2)}, u32[]{:S(2)}) collective-permute-start(f32[2,12,12,256]{3,2,1,0:T(8,128)S(1)} %get-tuple-element.28), channel_id=1, source_target_pairs={{0,32},{32,64},{64,96},{96,128},{128,160},{160,192},{192,224},{224... | collective-permute-start | bytes 884744 | tf_op jit(solution)/shard_map/ppermute | solution.py:13
  28.2 21.3 %copy-start.44 = (s32[3]{0:T(128)S(1)}, s32[3]{0:T(128)}, u32[]{:S(2)}) copy-start(s32[3]{0:T(128)} %param.17) | copy-start | bytes 40
  28.2 51.2 %collective-permute-start = (f32[2,12,12,256]{3,2,1,0:T(8,128)}, f32[2,12,12,256]{3,2,1,0:T(8,128)S(1)}, u32[]{:S(2)}, u32[]{:S(2)}) collective-permute-start(f32[2,12,12,256]{3,2,1,0:T(8,128)} %convolution_add_fusion.3), channel_id=1, source_target_pairs={{0,32},{32,64},{64,96},{96,128},{128,160},{160,192},{192,224},{224... | collective-permute-start | bytes 884744 | tf_op jit(solution)/shard_map/ppermute | solution.py:13
  46.3 12.4 %copy-start.38 = (f32[2,32]{1,0:T(2,128)}, f32[2,32]{1,0:T(2,128)S(1)}, u32[]{:S(2)}) copy-start(f32[2,32]{1,0:T(2,128)S(1)} %reduce_sum.554) | copy-start | bytes 772
  64.7 6.0 %copy-start.12 = (bf16[3,3,256,256]{3,2,1,0:T(8,128)(2,1)S(1)}, bf16[3,3,256,256]{3,2,1,0:T(8,128)(2,1)}, u32[]{:S(2)}) copy-start(bf16[3,3,256,256]{3,2,1,0:T(8,128)(2,1)} %copy.35) | copy-start | bytes 3538948
  64.7 6.0 %copy-start.24 = (f32[1,256]{1,0:T(1,128)S(1)}, f32[1,256]{1,0:T(1,128)}, u32[]{:S(2)}) copy-start(f32[1,256]{1,0:T(1,128)} %param.23) | copy-start | bytes 3076
  64.7 6.0 %copy-start.28 = (f32[1,256]{1,0:T(1,128)S(1)}, f32[1,256]{1,0:T(1,128)}, u32[]{:S(2)}) copy-start(f32[1,256]{1,0:T(1,128)} %param.22) | copy-start | bytes 3076
  64.7 6.0 %copy-start.32 = (f32[2,256]{1,0:T(2,128)S(1)}, f32[2,256]{1,0:T(2,128)}, u32[]{:S(2)}) copy-start(f32[2,256]{1,0:T(2,128)} %mul.483) | copy-start | bytes 6148
  76.6 26.7 %collective-permute-start.4 = (f32[2,12,12,256]{3,2,1,0:T(8,128)}, f32[2,12,12,256]{3,2,1,0:T(8,128)}, u32[]{:S(2)}, u32[]{:S(2)}) collective-permute-start(f32[2,12,12,256]{3,2,1,0:T(8,128)} %get-tuple-element.30), channel_id=1, source_target_pairs={{0,32},{32,64},{64,96},{96,128},{128,160},{160,192},{192,224},{224... | collective-permute-start | bytes 884744 | tf_op jit(solution)/shard_map/ppermute | solution.py:13
  81.6 21.7 %copy-start.11 = (bf16[1,2,12,12,256]{4,1,3,2,0:T(2,128)(2,1)S(1)}, bf16[1,2,12,12,256]{4,1,3,2,0:T(2,128)(2,1)}, u32[]{:S(2)}) copy-start(bf16[1,2,12,12,256]{4,1,3,2,0:T(2,128)(2,1)} %get-tuple-element.22) | copy-start | bytes 442372
  82.2 25.9 %copy-start.3 = (f32[2,12,12,256]{3,2,1,0:T(8,128)}, f32[2,12,12,256]{3,2,1,0:T(8,128)S(1)}, u32[]{:S(2)}) copy-start(f32[2,12,12,256]{3,2,1,0:T(8,128)S(1)} %convolution_add_fusion.2) | copy-start | bytes 884740
  82.2 42.5 %collective-permute-start.1 = (f32[2,12,12,256]{3,2,1,0:T(8,128)S(1)}, f32[2,12,12,256]{3,2,1,0:T(8,128)S(1)}, u32[]{:S(2)}, u32[]{:S(2)}) collective-permute-start(f32[2,12,12,256]{3,2,1,0:T(8,128)S(1)} %convolution_add_fusion.2), channel_id=1, source_target_pairs={{0,32},{32,64},{64,96},{96,128},{128,160},{160,192},{192,224},{224... | collective-permute-start | bytes 884744 | tf_op jit(solution)/shard_map/ppermute | solution.py:13
  105.1 6.7 %copy-start.25 = (f32[1,256]{1,0:T(1,128)S(1)}, f32[1,256]{1,0:T(1,128)}, u32[]{:S(2)}) copy-start(f32[1,256]{1,0:T(1,128)} %param.23) | copy-start | bytes 3076
  105.1 6.7 %copy-start.29 = (f32[1,256]{1,0:T(1,128)S(1)}, f32[1,256]{1,0:T(1,128)}, u32[]{:S(2)}) copy-start(f32[1,256]{1,0:T(1,128)} %param.22) | copy-start | bytes 3076
  105.1 6.7 %copy-start.33 = (f32[2,256]{1,0:T(2,128)S(1)}, f32[2,256]{1,0:T(2,128)}, u32[]{:S(2)}) copy-start(f32[2,256]{1,0:T(2,128)} %mul.504) | copy-start | bytes 6148
  105.8 6.0 %copy-start.13 = (bf16[3,3,256,256]{3,2,1,0:T(8,128)(2,1)S(1)}, bf16[3,3,256,256]{3,2,1,0:T(8,128)(2,1)}, u32[]{:S(2)}) copy-start(bf16[3,3,256,256]{3,2,1,0:T(8,128)(2,1)} %copy.35) | copy-start | bytes 3538948
  117.9 27.3 %collective-permute-start.5 = (f32[2,12,12,256]{3,2,1,0:T(8,128)}, f32[2,12,12,256]{3,2,1,0:T(8,128)}, u32[]{:S(2)}, u32[]{:S(2)}) collective-permute-start(f32[2,12,12,256]{3,2,1,0:T(8,128)} %get-tuple-element.32), channel_id=1, source_target_pairs={{0,32},{32,64},{64,96},{96,128},{128,160},{160,192},{192,224},{224... | collective-permute-start | bytes 884744 | tf_op jit(solution)/shard_map/ppermute | solution.py:13
  147.2 6.0 %copy-start.14 = (bf16[3,3,256,256]{3,2,1,0:T(8,128)(2,1)S(1)}, bf16[3,3,256,256]{3,2,1,0:T(8,128)(2,1)}, u32[]{:S(2)}) copy-start(bf16[3,3,256,256]{3,2,1,0:T(8,128)(2,1)} %copy.35) | copy-start | bytes 3538948
  147.2 6.0 %copy-start.26 = (f32[1,256]{1,0:T(1,128)S(1)}, f32[1,256]{1,0:T(1,128)}, u32[]{:S(2)}) copy-start(f32[1,256]{1,0:T(1,128)} %param.23) | copy-start | bytes 3076
  147.2 6.0 %copy-start.30 = (f32[1,256]{1,0:T(1,128)S(1)}, f32[1,256]{1,0:T(1,128)}, u32[]{:S(2)}) copy-start(f32[1,256]{1,0:T(1,128)} %param.22) | copy-start | bytes 3076
  147.2 6.0 %copy-start.34 = (f32[2,256]{1,0:T(2,128)S(1)}, f32[2,256]{1,0:T(2,128)}, u32[]{:S(2)}) copy-start(f32[2,256]{1,0:T(2,128)} %mul.525) | copy-start | bytes 6148
  153.2 4.7 %copy-start.10 = (bf16[1,2,12,12,256]{4,1,3,2,0:T(2,128)(2,1)S(1)}, bf16[1,2,12,12,256]{4,1,3,2,0:T(2,128)(2,1)}, u32[]{:S(2)}) copy-start(bf16[1,2,12,12,256]{4,1,3,2,0:T(2,128)(2,1)} %get-tuple-element.21) | copy-start | bytes 442372
  183.2 4.0 copy-start.17
  183.2 4.0 copy-start.18
  194.3 25.2 %collective-permute-start.2 = (f32[2,12,12,256]{3,2,1,0:T(8,128)S(1)}, f32[2,12,12,256]{3,2,1,0:T(8,128)S(1)}, u32[]{:S(2)}, u32[]{:S(2)}) collective-permute-start(f32[2,12,12,256]{3,2,1,0:T(8,128)S(1)} %convolution_add_fusion.1), channel_id=1, source_target_pairs={{0,32},{32,64},{64,96},{96,128},{128,160},{160,192},{192,224},{224... | collective-permute-start | bytes 884744 | tf_op jit(solution)/shard_map/ppermute | solution.py:13
  (20 other events, 40.8 us)
Sparse Core Ops, SparseCore 0:
  192.0 255.0 reduce-scatter.1
where the time goes:
time: 455 us; the launch traced here: 454 us
  waiting for transfers between devices  280 us (62%)
  local copies, waits for them, and re-layouts  88.7 us (19%)
  starting transfers between devices  26 us (6%)
  between operations  21 us (5%)
  other arithmetic  19.8 us (4%)
  matrix products  18.8 us (4%)
    reduce_scatter x1, waiting for transfers between devices, shards(): shard_sum = lax.psum_scatter(total, 'dp', scatter_dimension=0, tiled=True)  222 us
    ppermute x6, waiting for transfers between devices, passed_along(): return lax.ppermute(block, axis, route)  57.9 us
    unnamed x182, local copies, waits for them, and re-layouts  50 us
    ppermute x6, starting transfers between devices, passed_along(): return lax.ppermute(block, axis, route)  25.9 us
    reshape x4, local copies, waits for them, and re-layouts, patches(): return jnp.concatenate(shifted, axis=-1).reshape(-1, 9 * images.shape[3])  12.8 us
    dot_general x4, matrix products, backward_layer(): jnp.dot(patches(narrow), flipped(weight), preferred_element_type=jnp.floa...  10.8 us
  transfers between devices with their start and end apart: 7, of which 5 were waited for; matrix products, arithmetic and copies ran while one was open for 14% of the time, Pallas kernels for 0%

commit v1 on v0

v1 whole, which is shorter than its diff:
```python
import jax
import jax.numpy as jnp
from jax import lax
from jax.experimental import pallas as pl
from jax.experimental.pallas import tpu as pltpu
from jax.sharding import PartitionSpec as P

C = 256
TAPS = 9
SIDE = 12
PAD = 16
IMAGES = 2
LINES = IMAGES * SIDE
ROWS = LINES * PAD
PACKED = LINES * SIDE
TICKS = 4
SECTIONS = 16
GROUP = 8
NY = 4
NZ = 8
BLOCK = 72
PARTS = 3
PIECE = BLOCK // PARTS
EPS = 1e-05
COUNT = SIDE * SIDE * GROUP
BATCH = 64
MESH = pl.DeviceIdType.MESH
F32 = jnp.float32
BF16 = jnp.bfloat16


def group_mean(columns):
    lane = lax.broadcasted_iota(jnp.int32, columns.shape, 1)
    for step in (1, 2, 4):
        below = pltpu.roll(columns, step, 1)
        above = pltpu.roll(columns, C - step, 1)
        columns = columns + jnp.where((lane & step) == 0, above, below)
    return columns * (1.0 / COUNT)


def per_image(values):
    return jnp.sum(values.reshape(IMAGES, SIDE * PAD, C), axis=1)


def spread_out(columns):
    return jnp.broadcast_to(columns[:, None, :], (IMAGES, SIDE * PAD, C)).reshape(ROWS, C)


def normed(values, inside):
    average = spread_out(group_mean(per_image(jnp.where(inside, values, 0.0))))
    centred = jnp.where(inside, values - average, 0.0)
    spread = group_mean(per_image(centred * centred))
    scale = lax.rsqrt(spread + EPS)
    return centred * spread_out(scale), scale


def kernel(
    order_ref,
    act_ref,
    fresh_act_ref,
    saved_ref,
    grad_ref,
    fresh_grad_ref,
    fw_ref,
    fgain_ref,
    fbias_ref,
    bw_ref,
    bgain_ref,
    bbias_ref,
    emitted_ref,
    returned_ref,
    wgrad_ref,
    x_buf,
    e_buf,
    xhat_buf,
    slope_buf,
    scale_buf,
    turned_buf,
    bwt_buf,
    hp_buf,
    ep_buf,
    total_buf,
    act_out,
    act_in,
    grad_out,
    grad_in,
    y_in,
    y_sum,
    z_in,
    act_send,
    act_recv,
    grad_send,
    grad_recv,
    y_send,
    y_recv,
    z_send,
    z_recv,
):
    section = lax.axis_index("section")
    shard = lax.axis_index("dp")
    my_y = shard // NZ
    my_z = lax.rem(shard, NZ)

    barrier = pltpu.get_barrier_semaphore()
    for near in (lax.rem(section + 1, SECTIONS), lax.rem(section + SECTIONS - 1, SECTIONS)):
        pl.semaphore_signal(
            barrier, inc=1, device_id={"section": near, "dp": shard}, device_id_type=MESH
        )
    for k in range(1, NY):
        peer = lax.rem(my_y + k, NY) * NZ + my_z
        pl.semaphore_signal(
            barrier, inc=1, device_id={"section": section, "dp": peer}, device_id_type=MESH
        )
    for k in range(1, NZ):
        peer = my_y * NZ + lax.rem(my_z + k, NZ)
        pl.semaphore_signal(
            barrier, inc=1, device_id={"section": section, "dp": peer}, device_id_type=MESH
        )

    place = lax.broadcasted_iota(jnp.int32, (ROWS, C), 0)
    inside = (place & (PAD - 1)) < SIDE
    low_half = lax.broadcasted_iota(jnp.int32, (LINES // 2, 8, C), 1) < 4

    x_buf[...] = jnp.zeros_like(x_buf)
    e_buf[...] = jnp.zeros_like(e_buf)
    hp_buf[...] = jnp.zeros_like(hp_buf)
    ep_buf[...] = jnp.zeros_like(ep_buf)

    def store_shifted(buf, values):
        for kc, moved in enumerate((pltpu.roll(values, 1, 0), values, pltpu.roll(values, ROWS - 1, 0))):
            buf[kc, :, 1 : SIDE + 1] = moved.astype(BF16).reshape(IMAGES, SIDE, PAD, C)

    def columns_of(buf):
        return jnp.concatenate(
            [
                buf[kc, :, kr : kr + SIDE].reshape(ROWS, C)
                for kr in range(3)
                for kc in range(3)
            ],
            axis=1,
        )

    def pack(out, values):
        lines = values.reshape(LINES // 2, 2, PAD, C)
        out[0:LINES] = lines[:, :, 0:8].reshape(LINES, 8, C)
        rest = lines[:, :, 8:16]
        second = pltpu.roll(rest[:, 1].reshape(LINES // 2 * 8, C), 4, 0).reshape(LINES // 2, 8, C)
        out[LINES : LINES + LINES // 2] = jnp.where(low_half, rest[:, 0], second)

    def unpack(buf, source):
        buf[:, 0:8] = source[0:LINES]
        rest = source[LINES : LINES + LINES // 2]
        down = pltpu.roll(rest.reshape(LINES // 2 * 8, C), LINES // 2 * 8 - 4, 0).reshape(
            LINES // 2, 8, C
        )
        both = jnp.where(low_half, rest, 0.0), jnp.where(low_half, down, 0.0)
        buf[:, 8:16] = jnp.stack(both, axis=1).reshape(LINES, 8, C)

    def sender(out, into, send, recv, tick):
        return pltpu.make_async_remote_copy(
            src_ref=out.at[tick],
            dst_ref=into.at[tick],
            send_sem=send.at[tick],
            recv_sem=recv.at[tick],
            device_id={"section": lax.rem(section + 1, SECTIONS), "dp": shard},
            device_id_type=MESH,
        )

    def send_on(*stream):
        @pl.when(section < SECTIONS - 1)
        def _():
            sender(*stream).start()

    def take(buf, fresh_ref, stream, tick):
        @pl.when(section == 0)
        def _():
            buf[:, 0:SIDE] = fresh_ref[order_ref[tick - 1]].astype(F32)

        @pl.when(section > 0)
        def _():
            sender(*stream).wait_recv()
            unpack(buf, stream[1].at[tick - 1])

    act_stream = lambda tick: (act_out, act_in, act_send, act_recv, tick)
    grad_stream = lambda tick: (grad_out, grad_in, grad_send, grad_recv, tick)

    def prepare(tick):
        x_buf[:, 0:SIDE] = saved_ref[tick].astype(F32)
        x_buf[:, SIDE:PAD] = jnp.zeros((LINES, PAD - SIDE, C), F32)
        xhat, scale = normed(x_buf[...].reshape(ROWS, C), inside)
        gain = bgain_ref[...]
        scaled = xhat * gain + bbias_ref[...]
        gate = 1.0 / (1.0 + jnp.exp(-scaled))
        hidden = jnp.where(inside, scaled * gate, 0.0)
        slope = gate * (1.0 + scaled * (1.0 - gate)) * gain
        xhat_buf[tick] = xhat
        slope_buf[tick] = jnp.where(inside, slope, 0.0)
        scale_buf[tick] = scale
        for kc, moved in enumerate((pltpu.roll(hidden, 1, 0), hidden, pltpu.roll(hidden, ROWS - 1, 0))):
            turned_buf[tick, kc * C : (kc + 1) * C] = moved.T.astype(BF16)

    def backward(tick):
        incoming = e_buf[...].reshape(ROWS, C)
        store_shifted(ep_buf, incoming)
        hidden_grad = jnp.dot(columns_of(ep_buf), bwt_buf[...], preferred_element_type=F32)
        through = hidden_grad * slope_buf[tick]
        xhat = xhat_buf[tick]
        level = spread_out(group_mean(per_image(through)))
        tilt = spread_out(group_mean(per_image(through * xhat)))
        result = incoming + spread_out(scale_buf[tick]) * (through - level - xhat * tilt)
        returned_ref[tick] = result.reshape(LINES, PAD, C)[:, 0:SIDE]
        return result

    def weight_terms(tick):
        for kr in range(3):
            shifted = ep_buf[1, :, 2 - kr : 2 - kr + SIDE].reshape(ROWS, C)
            term = jnp.dot(turned_buf[tick], shifted, preferred_element_type=F32)
            rows = pl.ds(kr * 3 * C, 3 * C)
            if tick == 0:
                total_buf[rows] = term
            else:
                total_buf[rows] += term

    def forward(tick):
        values = x_buf[...].reshape(ROWS, C)
        xhat, _ = normed(values, inside)
        scaled = xhat * fgain_ref[...] + fbias_ref[...]
        hidden = jnp.where(inside, scaled / (1.0 + jnp.exp(-scaled)), 0.0)
        store_shifted(hp_buf, hidden)
        result = values + jnp.dot(columns_of(hp_buf), fw_ref[...], preferred_element_type=F32)
        emitted_ref[tick] = result.reshape(LINES, PAD, C)[:, 0:SIDE]
        return result

    for kr in range(3):
        for kc in range(3):
            mirrored = ((2 - kr) * 3 + 2 - kc) * C
            bwt_buf[(kr * 3 + kc) * C : (kr * 3 + kc + 1) * C] = bw_ref[mirrored : mirrored + C].T

    prepare(0)
    e_buf[:, 0:SIDE] = grad_ref[...].astype(F32)
    result = backward(0)
    pack(grad_out.at[0], result)
    pl.semaphore_wait(barrier, 2 + NY - 1 + NZ - 1)
    send_on(*grad_stream(0))
    x_buf[:, 0:SIDE] = act_ref[...].astype(F32)
    pack(act_out.at[0], forward(0))
    send_on(*act_stream(0))
    weight_terms(0)
    for tick in range(1, TICKS):
        prepare(tick)

    take(e_buf, fresh_grad_ref, grad_stream(0), 1)
    pack(grad_out.at[1], backward(1))
    send_on(*grad_stream(1))
    weight_terms(1)
    take(x_buf, fresh_act_ref, act_stream(0), 1)
    pack(act_out.at[1], forward(1))

    take(e_buf, fresh_grad_ref, grad_stream(1), 2)
    pack(grad_out.at[2], backward(2))
    send_on(*grad_stream(2))
    send_on(*act_stream(1))
    weight_terms(2)

    take(e_buf, fresh_grad_ref, grad_stream(2), 3)
    backward(3)
    weight_terms(3)

    total = total_buf.reshape(NY, NZ, BLOCK, C)

    def y_copy(part, k):
        peer = lax.rem(my_y + k, NY)
        return pltpu.make_async_remote_copy(
            src_ref=total.at[peer, :, pl.ds(part * PIECE, PIECE)],
            dst_ref=y_in.at[part, NY - 1 - k],
            send_sem=y_send.at[part, k - 1],
            recv_sem=y_recv.at[part, NY - 1 - k],
            device_id={"section": section, "dp": peer * NZ + my_z},
            device_id_type=MESH,
        )

    def z_copy(part, k):
        peer = lax.rem(my_z + k, NZ)
        return pltpu.make_async_remote_copy(
            src_ref=y_sum.at[part, peer],
            dst_ref=z_in.at[part, NZ - 1 - k],
            send_sem=z_send.at[part, k - 1],
            recv_sem=z_recv.at[part, NZ - 1 - k],
            device_id={"section": section, "dp": my_y * NZ + peer},
            device_id_type=MESH,
        )

    for part in range(PARTS):
        for k in (2, 1, 3):
            y_copy(part, k).start()

    take(x_buf, fresh_act_ref, act_stream(1), 2)
    pack(act_out.at[2], forward(2))
    send_on(*act_stream(2))

    for part in range(PARTS):
        for k in range(1, NY):
            y_copy(part, k).wait_recv()
        y_sum[part] = total[my_y, :, pl.ds(part * PIECE, PIECE)] + (
            y_in[part, 0] + y_in[part, 1] + y_in[part, 2]
        )
        for k in (4, 3, 5, 2, 6, 1, 7):
            z_copy(part, k).start()

    take(x_buf, fresh_act_ref, act_stream(2), 3)
    forward(3)

    for part in range(PARTS):
        for k in range(1, NZ):
            z_copy(part, k).wait_recv()
        block = y_sum[part, my_z]
        for k in range(NZ - 1):
            block = block + z_in[part, k]
        wgrad_ref[part * PIECE : (part + 1) * PIECE] = block * (1.0 / BATCH)

    @pl.when(section < SECTIONS - 1)
    def _():
        for tick in range(TICKS - 1):
            sender(*grad_stream(tick)).wait_send()
            sender(*act_stream(tick)).wait_send()

    for part in range(PARTS):
        for k in range(1, NY):
            y_copy(part, k).wait_send()
        for k in range(1, NZ):
            z_copy(part, k).wait_send()


def shards(
    arriving_activations,
    fresh_images,
    saved_inputs,
    arriving_gradients,
    fresh_gradients,
    feed_order,
    forward_weight,
    forward_gain,
    forward_bias,
    backward_weight,
    backward_gain,
    backward_bias,
):
    fold = (LINES, SIDE, C)
    vmem = pl.BlockSpec(memory_space=pltpu.VMEM)
    dma = pltpu.SemaphoreType.DMA
    relay = pltpu.VMEM((TICKS - 1, PACKED // 8, 8, C), F32)
    emitted, returned, block = pl.pallas_call(
        kernel,
        out_shape=(
            jax.ShapeDtypeStruct((TICKS,) + fold, F32),
            jax.ShapeDtypeStruct((TICKS,) + fold, F32),
            jax.ShapeDtypeStruct((BLOCK, C), F32),
        ),
        in_specs=[pl.BlockSpec(memory_space=pltpu.SMEM)] + [vmem] * 11,
        out_specs=(vmem, vmem, vmem),
        scratch_shapes=[
            pltpu.VMEM((LINES, PAD, C), F32),
            pltpu.VMEM((LINES, PAD, C), F32),
            pltpu.VMEM((TICKS, ROWS, C), F32),
            pltpu.VMEM((TICKS, ROWS, C), F32),
            pltpu.VMEM((TICKS, IMAGES, C), F32),
            pltpu.VMEM((TICKS, 3 * C, ROWS), BF16),
            pltpu.VMEM((TAPS * C, C), BF16),
            pltpu.VMEM((3, IMAGES, SIDE + 2, PAD, C), BF16),
            pltpu.VMEM((3, IMAGES, SIDE + 2, PAD, C), BF16),
            pltpu.VMEM((TAPS * C, C), F32),
            relay,
            relay,
            relay,
            relay,
            pltpu.VMEM((PARTS, NY - 1, NZ, PIECE, C), F32),
            pltpu.VMEM((PARTS, NZ, PIECE, C), F32),
            pltpu.VMEM((PARTS, NZ - 1, PIECE, C), F32),
            dma((TICKS - 1,)),
            dma((TICKS - 1,)),
            dma((TICKS - 1,)),
            dma((TICKS - 1,)),
            dma((PARTS, NY - 1)),
            dma((PARTS, NY - 1)),
            dma((PARTS, NZ - 1)),
            dma((PARTS, NZ - 1)),
        ],
        compiler_params=pltpu.CompilerParams(
            collective_id=0, has_side_effects=True, vmem_limit_bytes=60 * 1024 * 1024
        ),
    )(
        feed_order,
        arriving_activations.reshape(fold),
        fresh_images.reshape((TICKS - 1,) + fold),
        saved_inputs.reshape((TICKS,) + fold),
        arriving_gradients.reshape(fold),
        fresh_gradients.reshape((TICKS - 1,) + fold),
        forward_weight[0],
        forward_gain,
        forward_bias,
        backward_weight[0],
        backward_gain,
        backward_bias,
    )
    whole = (TICKS, 1, IMAGES, SIDE, SIDE, C)
    return (emitted.reshape(whole), returned.reshape(whole), block[None])


def solution(mesh):
    placed = (
        P("section", "dp", None, None, None),
        P(None, "dp", None, None, None),
        P(None, "section", "dp", None, None, None),
        P("section", "dp", None, None, None),
        P(None, "dp", None, None, None),
        P(),
        P("section", None, None),
        P("section", None),
        P("section", None),
        P("section", None, None),
        P("section", None),
        P("section", None),
    )
    return jax.shard_map(
        shards,
        mesh=mesh,
        in_specs=placed,
        out_specs=(
            P(None, "section", "dp", None, None, None),
            P(None, "section", "dp", None, None, None),
            P("section", "dp", None),
        ),
        check_vma=False,
    )
```

time: 455 us -> 146 us (0.32)
  waiting for transfers between devices: 280 us -> 0 us
  Pallas kernels: 0 us -> 132 us
  local copies, waits for them, and re-layouts: 88.7 us -> 13.4 us
  starting transfers between devices: 26 us -> 0 us
  between operations: 21 us -> 0.66 us
  other arithmetic: 19.8 us -> 0 us
  matrix products: 18.8 us -> 0 us
    reduce_scatter x1 -> x0, waiting for transfers between devices: 222 us -> none  [shards(): shard_sum = lax.psum_scatter(total, 'dp', scatter_dimension=0, tiled=True)]
    pallas_call x0 -> x1, Pallas kernels: none -> 132 us  [shards(): pl.pallas_call(kernel, out_shape=(jax.ShapeDtypeStruct((TICKS,) + fold, F...]
    ppermute x6 -> x0, waiting for transfers between devices: 57.9 us -> none  [passed_along(): return lax.ppermute(block, axis, route)]
    unnamed x182 -> x16, local copies, waits for them, and re-layouts: 50 us -> 13.4 us
    ppermute x6 -> x0, starting transfers between devices: 25.9 us -> none  [passed_along(): return lax.ppermute(block, axis, route)]
    dot_general x9 -> x0, matrix products: 18.8 us -> none  [the longest x4 10.8 us: backward_layer(): jnp.dot(patches(narrow), flipped(weight), preferred_element_type=jnp.floa...]
    reshape x8 -> x0, local copies, waits for them, and re-layouts: 14.9 us -> none  [the longest x4 12.8 us: patches(): return jnp.concatenate(shifted, axis=-1).reshape(-1, 9 * images.shape[3])]
    convert_element_type x11 -> x0, other arithmetic: 11 us -> none  [the longest x4 6.5 us: backward_layer(): hidden = activated.astype(jnp.bfloat16)]
  transfers between devices with their start and end apart: 7 -> 0, of which waited for: 5 -> 0; matrix products, arithmetic and copies ran while one was open for 14% -> 0% of each run, Pallas kernels for 0% -> 0%
where the time goes in v1:
time: 146 us
  Pallas kernels  132 us (90%)
  local copies, waits for them, and re-layouts  13.4 us (9%)
    pallas_call x1, Pallas kernels, shards(): pl.pallas_call(kernel, out_shape=(jax.ShapeDtypeStruct((TICKS,) + fold, F...  132 us
    unnamed x16, local copies, waits for them, and re-layouts  13.4 us

profile of v1, /device:TPU:4, one launch (start us, length us, event | category | flops | bytes accessed | tf_op | source)
XLA Modules:
  0.0 145.7 jit_solution(12511814964900604899)
XLA Ops:
  0.6 0.0 copy-start.2
  0.6 1.7 %copy.15 = bf16[1,2,12,12,256]{4,3,2,1,0:T(8,128)(2,1)} copy(bf16[1,2,12,12,256]{4,1,3,2,0:T(2,128)(2,1)} %param.12) | data formatting | bytes 294912 | tf_op args[0]
  2.3 0.0 copy-start.1
  2.3 1.7 %copy.18 = bf16[1,2,12,12,256]{4,3,2,1,0:T(8,128)(2,1)} copy(bf16[1,2,12,12,256]{4,1,3,2,0:T(2,128)(2,1)} %param.15) | data formatting | bytes 294912 | tf_op args[3]
  4.0 1.9 %copy.16 = bf16[3,2,12,12,256]{4,3,2,1,0:T(8,128)(2,1)} copy(bf16[3,2,12,12,256]{4,1,3,2,0:T(2,128)(2,1)} %param.13) | data formatting | bytes 884736 | tf_op args[1]
  5.9 0.0 copy-done.2
  5.9 0.9 copy.19
  6.8 0.0 copy-done.1
  6.8 1.0 copy.17
  7.8 131.6 %shard_map.139 = (f32[4,24,12,256]{3,2,1,0:T(8,128)}, f32[4,24,12,256]{3,2,1,0:T(8,128)}, f32[72,256]{1,0:T(8,128)}) custom-call(s32[3]{0:T(128)} %order_ref.1, bf16[24,12,256]{2,1,0:T(8,128)(2,1)} %bitcast.17, bf16[3,24,12,256]{3,2,1,0:T(8,128)(2,1)} %bitcast.11, bf16[4,24,12,256]{3,2,1,0:T(8,128)(2,1)} %bitcast.10, bf16[24,12,256]{2,1,0:T(8,128)(2,1)} %bitcast.18, ...), custom_call_target="tpu_custom_call" | custom-call | tf_op jit(solution)/shard_map/pallas_call | solution.py:352
  139.4 0.0 copy-start
  139.4 3.6 %copy.20 = f32[4,1,2,12,12,256]{5,2,4,3,1,0:T(2,128)} copy(f32[4,1,2,12,12,256]{5,4,3,2,0,1:T(8,128)} %bitcast.14) | data formatting | bytes 2359296
  143.0 0.0 copy-done
  143.0 0.0 copy-start.3
  143.0 2.0 %copy.21 = f32[4,1,2,12,12,256]{5,2,4,3,1,0:T(2,128)} copy(f32[4,1,2,12,12,256]{5,4,3,2,0,1:T(8,128)S(1)} %bitcast.13) | data formatting | bytes 2359296
  145.0 0.0 copy-done.3
  145.0 0.6 copy.23
Async XLA Ops:
  0.6 5.3 %copy-start.2 = (bf16[3,2,12,12,256]{4,1,3,2,0:T(2,128)(2,1)S(1)}, bf16[3,2,12,12,256]{4,1,3,2,0:T(2,128)(2,1)}, u32[]{:S(2)}) copy-start(bf16[3,2,12,12,256]{4,1,3,2,0:T(2,128)(2,1)} %param.16) | copy-start | bytes 1327108
  2.3 4.5 %copy-start.1 = (bf16[4,1,2,12,12,256]{5,2,4,3,1,0:T(2,128)(2,1)S(1)}, bf16[4,1,2,12,12,256]{5,2,4,3,1,0:T(2,128)(2,1)}, u32[]{:S(2)}) copy-start(bf16[4,1,2,12,12,256]{5,2,4,3,1,0:T(2,128)(2,1)} %param.14) | copy-start | bytes 1769476
  139.4 3.6 %copy-start = (f32[4,24,12,256]{3,2,1,0:T(8,128)S(1)}, f32[4,24,12,256]{3,2,1,0:T(8,128)}, u32[]{:S(2)}) copy-start(f32[4,24,12,256]{3,2,1,0:T(8,128)} %get-tuple-element.7) | copy-start | bytes 3538948
  143.0 2.0 %copy-start.3 = (f32[72,256]{1,0:T(8,128)S(1)}, f32[72,256]{1,0:T(8,128)}, u32[]{:S(2)}) copy-start(f32[72,256]{1,0:T(8,128)} %get-tuple-element.8) | copy-start | bytes 221188

commit v2 on v1

v2 whole, which is shorter than its diff:
```python
import jax
import jax.numpy as jnp
from jax import lax
from jax.experimental import pallas as pl
from jax.experimental.pallas import tpu as pltpu
from jax.sharding import PartitionSpec as P

C = 256
HALF = 128
TAPS = 9
SIDE = 12
IMAGES = 2
PIXELS = SIDE * SIDE
NATIVE = PIXELS * 2 * IMAGES
ROWS = PIXELS * IMAGES
LINE = SIDE * 2 * IMAGES
TILES = ROWS // 8
TICKS = 4
SECTIONS = 16
GROUP = 8
NY = 4
NZ = 8
BLOCK = 72
PARTS = 3
PIECE = BLOCK // PARTS
EPS = 1e-05
COUNT = PIXELS * GROUP
BATCH = 64
MESH = pl.DeviceIdType.MESH
F32 = jnp.float32
BF16 = jnp.bfloat16


def even_pairs(shape):
    return (lax.broadcasted_iota(jnp.int32, shape, 0) & 2) == 0


def worked(native):
    upper, lower = native[:ROWS], native[ROWS:]
    even = even_pairs(upper.shape)
    first = jnp.where(even, upper, pltpu.roll(lower, 2, 0))
    second = jnp.where(even, pltpu.roll(upper, ROWS - 2, 0), lower)
    return jnp.concatenate([first, second], axis=1)


def stored(values):
    first, second = values[:, :HALF], values[:, HALF:]
    even = even_pairs(first.shape)
    upper = jnp.where(even, first, pltpu.roll(second, 2, 0))
    lower = jnp.where(even, pltpu.roll(first, ROWS - 2, 0), second)
    return jnp.concatenate([upper, lower], axis=0)


def group_mean(values):
    sums = jnp.sum(values, axis=0)
    sums = sums + pltpu.roll(sums, 4, 0)
    sums = sums + pltpu.roll(sums, 2, 0)
    lane = lax.broadcasted_iota(jnp.int32, sums.shape, 1)
    for step in (1, 2, 4):
        below = pltpu.roll(sums, step, 1)
        above = pltpu.roll(sums, C - step, 1)
        sums = sums + jnp.where((lane & step) == 0, above, below)
    return sums * (1.0 / COUNT)


def normed(values):
    centred = values - group_mean(values)
    scale = lax.rsqrt(group_mean(centred * centred) + EPS)
    return centred * scale, scale


def sideways(values):
    tiles = (SIDE // 2, SIDE // 2, 8, C)
    early = lax.broadcasted_iota(jnp.int32, (SIDE // 2, 1, 8, C), 2) < 4
    left = pltpu.roll(values, 4, 0).reshape(tiles)
    left = jnp.concatenate([jnp.where(early, 0.0, left[:, :1]), left[:, 1:]], axis=1)
    right = pltpu.roll(values, ROWS - 4, 0).reshape(tiles)
    right = jnp.concatenate([right[:, :-1], jnp.where(early, right[:, -1:], 0.0)], axis=1)
    return left.reshape(ROWS, C), values, right.reshape(ROWS, C)


def bordered(values):
    even = even_pairs((LINE, C))
    above = jnp.where(even, 0.0, pltpu.roll(values[ROWS - LINE :], 2, 0))
    below = jnp.where(even, pltpu.roll(values[:LINE], LINE - 2, 0), 0.0)
    return jnp.concatenate([above, values, below], axis=0).astype(BF16)


def columns_of(sides):
    return jnp.concatenate(
        [side[kr * LINE : kr * LINE + ROWS] for kr in range(3) for side in sides], axis=1
    )


def kernel(
    order_ref,
    act_ref,
    fresh_act_ref,
    saved_ref,
    grad_ref,
    fresh_grad_ref,
    fw_ref,
    fgain_ref,
    fbias_ref,
    bw_ref,
    bgain_ref,
    bbias_ref,
    emitted_ref,
    returned_ref,
    wgrad_ref,
    x_buf,
    e_buf,
    xhat_buf,
    slope_buf,
    scale_buf,
    hidden_buf,
    turned_buf,
    bwt_buf,
    border_buf,
    total_buf,
    act_out,
    act_in,
    grad_out,
    grad_in,
    y_in,
    y_sum,
    z_in,
    act_send,
    act_recv,
    grad_send,
    grad_recv,
    y_send,
    y_recv,
    z_send,
    z_recv,
):
    section = lax.axis_index("section")
    shard = lax.axis_index("dp")
    my_y = shard // NZ
    my_z = lax.rem(shard, NZ)

    barrier = pltpu.get_barrier_semaphore()
    for near in (lax.rem(section + 1, SECTIONS), lax.rem(section + SECTIONS - 1, SECTIONS)):
        pl.semaphore_signal(
            barrier, inc=1, device_id={"section": near, "dp": shard}, device_id_type=MESH
        )
    for k in range(1, NY):
        peer = lax.rem(my_y + k, NY) * NZ + my_z
        pl.semaphore_signal(
            barrier, inc=1, device_id={"section": section, "dp": peer}, device_id_type=MESH
        )
    for k in range(1, NZ):
        peer = my_y * NZ + lax.rem(my_z + k, NZ)
        pl.semaphore_signal(
            barrier, inc=1, device_id={"section": section, "dp": peer}, device_id_type=MESH
        )

    def sender(out, into, send, recv, tick):
        return pltpu.make_async_remote_copy(
            src_ref=out.at[tick],
            dst_ref=into.at[tick],
            send_sem=send.at[tick],
            recv_sem=recv.at[tick],
            device_id={"section": lax.rem(section + 1, SECTIONS), "dp": shard},
            device_id_type=MESH,
        )

    def send_on(*stream):
        @pl.when(section < SECTIONS - 1)
        def _():
            sender(*stream).start()

    def take(buf, fresh_ref, stream, tick):
        @pl.when(section == 0)
        def _():
            buf[...] = worked(fresh_ref[order_ref[tick - 1]].astype(F32)).reshape(TILES, 8, C)

        @pl.when(section > 0)
        def _():
            sender(*stream).wait_recv()
            buf[...] = stream[1][tick - 1]

    act_stream = lambda tick: (act_out, act_in, act_send, act_recv, tick)
    grad_stream = lambda tick: (grad_out, grad_in, grad_send, grad_recv, tick)

    def prepare(tick):
        values = worked(saved_ref[tick].astype(F32)).reshape(TILES, 8, C)
        xhat, scale = normed(values)
        gain = bgain_ref[...]
        scaled = xhat * gain + bbias_ref[...]
        gate = 1.0 / (1.0 + jnp.exp(-scaled))
        xhat_buf[tick] = xhat
        scale_buf[tick] = scale
        slope_buf[tick] = gate * (1.0 + scaled * (1.0 - gate)) * gain
        hidden_buf[tick] = scaled * gate

    def turn(tick):
        for kc, side in enumerate(sideways(hidden_buf[tick].reshape(ROWS, C))):
            turned_buf[tick, kc * C : (kc + 1) * C] = side.T.astype(BF16)

    def backward(tick):
        incoming = e_buf[...]
        sides = [bordered(side) for side in sideways(incoming.reshape(ROWS, C))]
        border_buf[...] = sides[1]
        hidden_grad = jnp.dot(columns_of(sides), bwt_buf[...], preferred_element_type=F32)
        through = hidden_grad.reshape(TILES, 8, C) * slope_buf[tick]
        xhat = xhat_buf[tick]
        level = group_mean(through)
        tilt = group_mean(through * xhat)
        return incoming + scale_buf[tick] * (through - level - xhat * tilt)

    def weight_terms(tick):
        for kr in range(3):
            shifted = border_buf[(2 - kr) * LINE : (2 - kr) * LINE + ROWS]
            term = jnp.dot(turned_buf[tick], shifted, preferred_element_type=F32)
            rows = pl.ds(kr * 3 * C, 3 * C)
            if tick == 0:
                total_buf[rows] = term
            else:
                total_buf[rows] += term

    def forward():
        values = x_buf[...]
        xhat, _ = normed(values)
        scaled = xhat * fgain_ref[...] + fbias_ref[...]
        hidden = scaled / (1.0 + jnp.exp(-scaled))
        sides = [bordered(side) for side in sideways(hidden.reshape(ROWS, C))]
        mixed = jnp.dot(columns_of(sides), fw_ref[...], preferred_element_type=F32)
        return values + mixed.reshape(TILES, 8, C)

    def store(out_ref, tick, values):
        out_ref[tick] = stored(values.reshape(ROWS, C))

    for kr in range(3):
        for kc in range(3):
            mirrored = ((2 - kr) * 3 + 2 - kc) * C
            bwt_buf[(kr * 3 + kc) * C : (kr * 3 + kc + 1) * C] = bw_ref[mirrored : mirrored + C].T

    prepare(0)
    e_buf[...] = worked(grad_ref[...].astype(F32)).reshape(TILES, 8, C)
    grad_out[0] = backward(0)
    pl.semaphore_wait(barrier, 2 + NY - 1 + NZ - 1)
    send_on(*grad_stream(0))
    x_buf[...] = worked(act_ref[...].astype(F32)).reshape(TILES, 8, C)
    act_out[0] = forward()
    send_on(*act_stream(0))
    for tick in range(1, TICKS):
        prepare(tick)
    store(returned_ref, 0, grad_out[0])
    store(emitted_ref, 0, act_out[0])
    turn(0)
    weight_terms(0)

    take(e_buf, fresh_grad_ref, grad_stream(0), 1)
    grad_out[1] = backward(1)
    send_on(*grad_stream(1))
    store(returned_ref, 1, grad_out[1])
    turn(1)
    weight_terms(1)
    take(x_buf, fresh_act_ref, act_stream(0), 1)
    act_out[1] = forward()
    store(emitted_ref, 1, act_out[1])
    turn(2)
    turn(3)

    take(e_buf, fresh_grad_ref, grad_stream(1), 2)
    grad_out[2] = backward(2)
    send_on(*grad_stream(2))
    send_on(*act_stream(1))
    store(returned_ref, 2, grad_out[2])
    weight_terms(2)

    take(e_buf, fresh_grad_ref, grad_stream(2), 3)
    store(returned_ref, 3, backward(3))
    weight_terms(3)

    total = total_buf.reshape(NY, NZ, BLOCK, C)

    def y_copy(part, k):
        peer = lax.rem(my_y + k, NY)
        return pltpu.make_async_remote_copy(
            src_ref=total.at[peer, :, pl.ds(part * PIECE, PIECE)],
            dst_ref=y_in.at[part, NY - 1 - k],
            send_sem=y_send.at[part, k - 1],
            recv_sem=y_recv.at[part, NY - 1 - k],
            device_id={"section": section, "dp": peer * NZ + my_z},
            device_id_type=MESH,
        )

    def z_copy(part, k):
        peer = lax.rem(my_z + k, NZ)
        return pltpu.make_async_remote_copy(
            src_ref=y_sum.at[part, peer],
            dst_ref=z_in.at[part, NZ - 1 - k],
            send_sem=z_send.at[part, k - 1],
            recv_sem=z_recv.at[part, NZ - 1 - k],
            device_id={"section": section, "dp": my_y * NZ + peer},
            device_id_type=MESH,
        )

    for part in range(PARTS):
        for k in (2, 1, 3):
            y_copy(part, k).start()

    take(x_buf, fresh_act_ref, act_stream(1), 2)
    act_out[2] = forward()
    send_on(*act_stream(2))
    store(emitted_ref, 2, act_out[2])

    for part in range(PARTS):
        for k in range(1, NY):
            y_copy(part, k).wait_recv()
        y_sum[part] = total[my_y, :, pl.ds(part * PIECE, PIECE)] + (
            y_in[part, 0] + y_in[part, 1] + y_in[part, 2]
        )
        for k in (4, 3, 5, 2, 6, 1, 7):
            z_copy(part, k).start()

    take(x_buf, fresh_act_ref, act_stream(2), 3)
    store(emitted_ref, 3, forward())

    for part in range(PARTS):
        for k in range(1, NZ):
            z_copy(part, k).wait_recv()
        block = y_sum[part, my_z]
        for k in range(NZ - 1):
            block = block + z_in[part, k]
        wgrad_ref[part * PIECE : (part + 1) * PIECE] = block * (1.0 / BATCH)

    @pl.when(section < SECTIONS - 1)
    def _():
        for tick in range(TICKS - 1):
            sender(*grad_stream(tick)).wait_send()
            sender(*act_stream(tick)).wait_send()

    for part in range(PARTS):
        for k in range(1, NY):
            y_copy(part, k).wait_send()
        for k in range(1, NZ):
            z_copy(part, k).wait_send()


def as_rows(images):
    lead = images.shape[:-4]
    n = len(lead)
    split = images.reshape(lead + (IMAGES, SIDE, SIDE, 2, HALF))
    turned = split.transpose(tuple(range(n)) + (n + 1, n + 2, n + 3, n, n + 4))
    return turned.reshape(lead + (NATIVE, HALF))


def as_images(rows):
    lead = rows.shape[:-2]
    n = len(lead)
    split = rows.reshape(lead + (SIDE, SIDE, 2, IMAGES, HALF))
    turned = split.transpose(tuple(range(n)) + (n + 3, n, n + 1, n + 2, n + 4))
    return turned.reshape(lead + (IMAGES, SIDE, SIDE, C))


def shards(
    arriving_activations,
    fresh_images,
    saved_inputs,
    arriving_gradients,
    fresh_gradients,
    feed_order,
    forward_weight,
    forward_gain,
    forward_bias,
    backward_weight,
    backward_gain,
    backward_bias,
):
    vmem = pl.BlockSpec(memory_space=pltpu.VMEM)
    dma = pltpu.SemaphoreType.DMA
    tile = (TILES, 8, C)
    relay = pltpu.VMEM((TICKS - 1,) + tile, F32)
    emitted, returned, block = pl.pallas_call(
        kernel,
        out_shape=(
            jax.ShapeDtypeStruct((TICKS, NATIVE, HALF), F32),
            jax.ShapeDtypeStruct((TICKS, NATIVE, HALF), F32),
            jax.ShapeDtypeStruct((BLOCK, C), F32),
        ),
        in_specs=[pl.BlockSpec(memory_space=pltpu.SMEM)] + [vmem] * 11,
        out_specs=(vmem, vmem, vmem),
        scratch_shapes=[
            pltpu.VMEM(tile, F32),
            pltpu.VMEM(tile, F32),
            pltpu.VMEM((TICKS,) + tile, F32),
            pltpu.VMEM((TICKS,) + tile, F32),
            pltpu.VMEM((TICKS, 8, C), F32),
            pltpu.VMEM((TICKS,) + tile, F32),
            pltpu.VMEM((TICKS, 3 * C, ROWS), BF16),
            pltpu.VMEM((TAPS * C, C), BF16),
            pltpu.VMEM((ROWS + 2 * LINE, C), BF16),
            pltpu.VMEM((TAPS * C, C), F32),
            relay,
            relay,
            relay,
            relay,
            pltpu.VMEM((PARTS, NY - 1, NZ, PIECE, C), F32),
            pltpu.VMEM((PARTS, NZ, PIECE, C), F32),
            pltpu.VMEM((PARTS, NZ - 1, PIECE, C), F32),
            dma((TICKS - 1,)),
            dma((TICKS - 1,)),
            dma((TICKS - 1,)),
            dma((TICKS - 1,)),
            dma((PARTS, NY - 1)),
            dma((PARTS, NY - 1)),
            dma((PARTS, NZ - 1)),
            dma((PARTS, NZ - 1)),
        ],
        compiler_params=pltpu.CompilerParams(
            collective_id=0, has_side_effects=True, vmem_limit_bytes=60 * 1024 * 1024
        ),
    )(
        feed_order,
        as_rows(arriving_activations[0]),
        as_rows(fresh_images),
        as_rows(saved_inputs[:, 0]),
        as_rows(arriving_gradients[0]),
        as_rows(fresh_gradients),
        forward_weight[0],
        forward_gain,
        forward_bias,
        backward_weight[0],
        backward_gain,
        backward_bias,
    )
    return (as_images(emitted)[:, None], as_images(returned)[:, None], block[None])


def solution(mesh):
    placed = (
        P("section", "dp", None, None, None),
        P(None, "dp", None, None, None),
        P(None, "section", "dp", None, None, None),
        P("section", "dp", None, None, None),
        P(None, "dp", None, None, None),
        P(),
        P("section", None, None),
        P("section", None),
        P("section", None),
        P("section", None, None),
        P("section", None),
        P("section", None),
    )
    return jax.shard_map(
        shards,
        mesh=mesh,
        in_specs=placed,
        out_specs=(
            P(None, "section", "dp", None, None, None),
            P(None, "section", "dp", None, None, None),
            P("section", "dp", None),
        ),
        check_vma=False,
    )
```

time: 146 us -> 135 us (0.925)
  local copies, waits for them, and re-layouts: 13.4 us -> 4.49 us
  Pallas kernels: 132 us -> 130 us
    unnamed x16 -> x7, local copies, waits for them, and re-layouts: 13.4 us -> 4.49 us
where the time goes in v2:
time: 135 us
  Pallas kernels  130 us (96%)
  local copies, waits for them, and re-layouts  4.49 us (3%)
    pallas_call x1, Pallas kernels, shards(): pl.pallas_call(kernel, out_shape=(jax.ShapeDtypeStruct((TICKS, NATIVE, HA...  130 us
    unnamed x7, local copies, waits for them, and re-layouts  4.49 us

profile of v2, /device:TPU:4, one launch (start us, length us, event | category | flops | bytes accessed | tf_op | source)
XLA Modules:
  0.0 135.3 jit_solution(7448384373671556895)
XLA Ops:
  0.6 130.2 %shard_map.139 = (f32[4,576,128]{2,1,0:T(8,128)}, f32[4,576,128]{2,1,0:T(8,128)}, f32[72,256]{1,0:T(8,128)}) custom-call(s32[3]{0:T(128)} %order_ref.1, bf16[576,128]{1,0:T(8,128)(2,1)} %bitcast.45, bf16[3,576,128]{2,1,0:T(8,128)(2,1)} %bitcast.43, bf16[4,576,128]{2,1,0:T(8,128)(2,1)} %bitcast.42, bf16[576,128]{1,0:T(8,128)(2,1)} %bitcast.46, ...), custom_call_target="tpu_custom_call" | custom-call | tf_op jit(solution)/shard_map/pallas_call | solution.py:377
  130.8 0.0 copy-start
  130.8 2.8 %copy.25 = f32[4,1,2,12,12,256]{5,2,4,3,1,0:T(2,128)} copy(f32[4,1,2,12,12,256]{5,2,4,3,1,0:T(2,128)} %bitcast.41) | data formatting | bytes 2359296
  133.7 0.0 copy-done
  133.7 0.0 copy-start.1
  133.7 1.0 copy.26
  134.7 0.0 copy-done.1
  134.7 0.6 copy.27
Async XLA Ops:
  130.8 2.8 %copy-start = (f32[4,576,128]{2,1,0:T(8,128)S(1)}, f32[4,576,128]{2,1,0:T(8,128)}, u32[]{:S(2)}) copy-start(f32[4,576,128]{2,1,0:T(8,128)} %get-tuple-element.7) | copy-start | bytes 3538948
  133.7 1.0 copy-start.1

commit v3 on v2

--- a/solution.py
+++ b/solution.py
@@ -20,6 +20,7 @@
 GROUP = 8
 NY = 4
 NZ = 8
+QUAD = 4
 BLOCK = 72
 PARTS = 3
 PIECE = BLOCK // PARTS
@@ -94,20 +95,29 @@
 
 def kernel(
     order_ref,
+    act_hbm,
+    fresh_act_hbm,
+    saved_hbm,
+    grad_hbm,
+    fresh_grad_hbm,
+    fw_hbm,
+    fgain_ref,
+    fbias_ref,
+    bw_hbm,
+    bgain_ref,
+    bbias_ref,
+    emitted_hbm,
+    returned_hbm,
+    wgrad_ref,
     act_ref,
     fresh_act_ref,
     saved_ref,
     grad_ref,
     fresh_grad_ref,
     fw_ref,
-    fgain_ref,
-    fbias_ref,
     bw_ref,
-    bgain_ref,
-    bbias_ref,
     emitted_ref,
     returned_ref,
-    wgrad_ref,
     x_buf,
     e_buf,
     xhat_buf,
@@ -125,6 +135,8 @@
     y_in,
     y_sum,
     z_in,
+    z_mid,
+    far_in,
     act_send,
     act_recv,
     grad_send,
@@ -133,11 +145,18 @@
     y_recv,
     z_send,
     z_recv,
+    far_send,
+    far_recv,
+    load_sem,
+    emitted_sem,
+    returned_sem,
 ):
     section = lax.axis_index("section")
     shard = lax.axis_index("dp")
     my_y = shard // NZ
     my_z = lax.rem(shard, NZ)
+    my_q = my_z // QUAD
+    my_w = lax.rem(my_z, QUAD)
 
     barrier = pltpu.get_barrier_semaphore()
     for near in (lax.rem(section + 1, SECTIONS), lax.rem(section + SECTIONS - 1, SECTIONS)):
@@ -149,11 +168,31 @@
         pl.semaphore_signal(
             barrier, inc=1, device_id={"section": section, "dp": peer}, device_id_type=MESH
         )
-    for k in range(1, NZ):
-        peer = my_y * NZ + lax.rem(my_z + k, NZ)
+    far = lax.rem(my_z + QUAD, NZ)
+    for peer in [my_q * QUAD + lax.rem(my_w + k, QUAD) for k in range(1, QUAD)] + [far]:
         pl.semaphore_signal(
-            barrier, inc=1, device_id={"section": section, "dp": peer}, device_id_type=MESH
-        )
+            barrier,
+            inc=1,
+            device_id={"section": section, "dp": my_y * NZ + peer},
+            device_id_type=MESH,
+        )
+
+    loads = [
+        pltpu.make_async_copy(source, buf, load_sem.at[i])
+        for i, (source, buf) in enumerate(
+            (
+                (bw_hbm, bw_ref),
+                (saved_hbm, saved_ref),
+                (grad_hbm, grad_ref),
+                (fw_hbm, fw_ref),
+                (act_hbm, act_ref),
+                (fresh_grad_hbm, fresh_grad_ref),
+                (fresh_act_hbm, fresh_act_ref),
+            )
+        )
+    ]
+    for load in loads:
+        load.start()
 
     def sender(out, into, send, recv, tick):
         return pltpu.make_async_remote_copy(
@@ -169,6 +208,11 @@
         @pl.when(section < SECTIONS - 1)
         def _():
             sender(*stream).start()
+
+    def sent(*stream):
+        @pl.when(section < SECTIONS - 1)
+        def _():
+            sender(*stream).wait_send()
 
     def take(buf, fresh_ref, stream, tick):
         @pl.when(section == 0)
@@ -228,50 +272,68 @@
         mixed = jnp.dot(columns_of(sides), fw_ref[...], preferred_element_type=F32)
         return values + mixed.reshape(TILES, 8, C)
 
-    def store(out_ref, tick, values):
-        out_ref[tick] = stored(values.reshape(ROWS, C))
-
+    def written(side, tick):
+        buf, out, sem = side
+        return pltpu.make_async_copy(buf.at[tick], out.at[tick], sem.at[tick])
+
+    def store(side, tick, values):
+        side[0][tick] = stored(values.reshape(ROWS, C))
+        written(side, tick).start()
+
+    emitted_side = (emitted_ref, emitted_hbm, emitted_sem)
+    returned_side = (returned_ref, returned_hbm, returned_sem)
+
+    loads[0].wait()
     for kr in range(3):
         for kc in range(3):
             mirrored = ((2 - kr) * 3 + 2 - kc) * C
             bwt_buf[(kr * 3 + kc) * C : (kr * 3 + kc + 1) * C] = bw_ref[mirrored : mirrored + C].T
 
+    loads[1].wait()
     prepare(0)
+    loads[2].wait()
     e_buf[...] = worked(grad_ref[...].astype(F32)).reshape(TILES, 8, C)
     grad_out[0] = backward(0)
-    pl.semaphore_wait(barrier, 2 + NY - 1 + NZ - 1)
-    send_on(*grad_stream(0))
+    loads[3].wait()
+    loads[4].wait()
     x_buf[...] = worked(act_ref[...].astype(F32)).reshape(TILES, 8, C)
     act_out[0] = forward()
-    send_on(*act_stream(0))
+    pl.semaphore_wait(barrier, 2 + NY - 1 + QUAD)
+    send_on(*grad_stream(0))
+    store(returned_side, 0, grad_out[0])
+    turn(0)
+    weight_terms(0)
     for tick in range(1, TICKS):
         prepare(tick)
-    store(returned_ref, 0, grad_out[0])
-    store(emitted_ref, 0, act_out[0])
-    turn(0)
-    weight_terms(0)
+    turn(1)
+    turn(2)
+    turn(3)
+    sent(*grad_stream(0))
+    send_on(*act_stream(0))
+    store(emitted_side, 0, act_out[0])
+    loads[5].wait()
+    loads[6].wait()
 
     take(e_buf, fresh_grad_ref, grad_stream(0), 1)
     grad_out[1] = backward(1)
+    sent(*act_stream(0))
     send_on(*grad_stream(1))
-    store(returned_ref, 1, grad_out[1])
-    turn(1)
+    store(returned_side, 1, grad_out[1])
     weight_terms(1)
     take(x_buf, fresh_act_ref, act_stream(0), 1)
     act_out[1] = forward()
-    store(emitted_ref, 1, act_out[1])
-    turn(2)
-    turn(3)
+    store(emitted_side, 1, act_out[1])
 
     take(e_buf, fresh_grad_ref, grad_stream(1), 2)
     grad_out[2] = backward(2)
     send_on(*grad_stream(2))
+    store(returned_side, 2, grad_out[2])
+    weight_terms(2)
+    sent(*grad_stream(2))
     send_on(*act_stream(1))
-    store(returned_ref, 2, grad_out[2])
-    weight_terms(2)
 
     take(e_buf, fresh_grad_ref, grad_stream(2), 3)
-    store(returned_ref, 3, backward(3))
+    store(returned_side, 3, backward(3))
     weight_terms(3)
 
     total = total_buf.reshape(NY, NZ, BLOCK, C)
@@ -288,56 +350,82 @@
         )
 
     def z_copy(part, k):
-        peer = lax.rem(my_z + k, NZ)
+        peer = lax.rem(my_w + k, QUAD)
         return pltpu.make_async_remote_copy(
-            src_ref=y_sum.at[part, peer],
-            dst_ref=z_in.at[part, NZ - 1 - k],
+            src_ref=y_sum.at[part, :, peer],
+            dst_ref=z_in.at[part, QUAD - 1 - k],
             send_sem=z_send.at[part, k - 1],
-            recv_sem=z_recv.at[part, NZ - 1 - k],
-            device_id={"section": section, "dp": my_y * NZ + peer},
+            recv_sem=z_recv.at[part, QUAD - 1 - k],
+            device_id={"section": section, "dp": my_y * NZ + my_q * QUAD + peer},
             device_id_type=MESH,
         )
 
-    for part in range(PARTS):
+    def far_copy(part):
+        return pltpu.make_async_remote_copy(
+            src_ref=z_mid.at[part, 1 - my_q],
+            dst_ref=far_in.at[part],
+            send_sem=far_send.at[part],
+            recv_sem=far_recv.at[part],
+            device_id={"section": section, "dp": my_y * NZ + far},
+            device_id_type=MESH,
+        )
+
+    def y_done(part):
+        for k in range(1, NY):
+            y_copy(part, k).wait_recv()
+        piece = total[my_y, :, pl.ds(part * PIECE, PIECE)] + (
+            y_in[part, 0] + y_in[part, 1] + y_in[part, 2]
+        )
+        y_sum[part] = piece.reshape(NZ // QUAD, QUAD, PIECE, C)
+        for k in (2, 1, 3):
+            z_copy(part, k).start()
+
+    def y_start(part):
+        if part > 0:
+            for k in range(1, NY):
+                y_copy(part - 1, k).wait_send()
         for k in (2, 1, 3):
             y_copy(part, k).start()
 
+    y_start(0)
     take(x_buf, fresh_act_ref, act_stream(1), 2)
     act_out[2] = forward()
+    sent(*act_stream(1))
     send_on(*act_stream(2))
-    store(emitted_ref, 2, act_out[2])
+    store(emitted_side, 2, act_out[2])
+    for part in range(1, PARTS):
+        y_start(part)
+        y_done(part - 1)
+
+    take(x_buf, fresh_act_ref, act_stream(2), 3)
+    store(emitted_side, 3, forward())
+
+    y_done(PARTS - 1)
 
     for part in range(PARTS):
-        for k in range(1, NY):
-            y_copy(part, k).wait_recv()
-        y_sum[part] = total[my_y, :, pl.ds(part * PIECE, PIECE)] + (
-            y_in[part, 0] + y_in[part, 1] + y_in[part, 2]
-        )
-        for k in (4, 3, 5, 2, 6, 1, 7):
-            z_copy(part, k).start()
-
-    take(x_buf, fresh_act_ref, act_stream(2), 3)
-    store(emitted_ref, 3, forward())
+        for k in range(1, QUAD):
+            z_copy(part, k).wait_recv()
+        z_mid[part] = y_sum[part, :, my_w] + (z_in[part, 0] + z_in[part, 1] + z_in[part, 2])
+        far_copy(part).start()
 
     for part in range(PARTS):
-        for k in range(1, NZ):
-            z_copy(part, k).wait_recv()
-        block = y_sum[part, my_z]
-        for k in range(NZ - 1):
-            block = block + z_in[part, k]
+        far_copy(part).wait_recv()
+        block = z_mid[part, my_q] + far_in[part]
         wgrad_ref[part * PIECE : (part + 1) * PIECE] = block * (1.0 / BATCH)
 
-    @pl.when(section < SECTIONS - 1)
-    def _():
-        for tick in range(TICKS - 1):
-            sender(*grad_stream(tick)).wait_send()
-            sender(*act_stream(tick)).wait_send()
-
+    for stream in (grad_stream(1), act_stream(2)):
+        sent(*stream)
+
+    for k in range(1, NY):
+        y_copy(PARTS - 1, k).wait_send()
     for part in range(PARTS):
-        for k in range(1, NY):
-            y_copy(part, k).wait_send()
-        for k in range(1, NZ):
+        for k in range(1, QUAD):
             z_copy(part, k).wait_send()
+        far_copy(part).wait_send()
+
+    for tick in range(TICKS):
+        written(emitted_side, tick).wait()
+        written(returned_side, tick).wait()
 
 
 def as_rows(images):
@@ -371,6 +459,7 @@
     backward_bias,
 ):
     vmem = pl.BlockSpec(memory_space=pltpu.VMEM)
+    whole = pl.BlockSpec(memory_space=pl.ANY)
     dma = pltpu.SemaphoreType.DMA
     tile = (TILES, 8, C)
     relay = pltpu.VMEM((TICKS - 1,) + tile, F32)
@@ -381,9 +470,22 @@
             jax.ShapeDtypeStruct((TICKS, NATIVE, HALF), F32),
             jax.ShapeDtypeStruct((BLOCK, C), F32),
         ),
-        in_specs=[pl.BlockSpec(memory_space=pltpu.SMEM)] + [vmem] * 11,
-        out_specs=(vmem, vmem, vmem),
+        in_specs=[pl.BlockSpec(memory_space=pltpu.SMEM)]
+        + [whole] * 6
+        + [vmem] * 2
+        + [whole]
+        + [vmem] * 2,
+        out_specs=(whole, whole, vmem),
         scratch_shapes=[
+            pltpu.VMEM((NATIVE, HALF), BF16),
+            pltpu.VMEM((TICKS - 1, NATIVE, HALF), BF16),
+            pltpu.VMEM((TICKS, NATIVE, HALF), BF16),
+            pltpu.VMEM((NATIVE, HALF), BF16),
+            pltpu.VMEM((TICKS - 1, NATIVE, HALF), BF16),
+            pltpu.VMEM((TAPS * C, C), BF16),
+            pltpu.VMEM((TAPS * C, C), BF16),
+            pltpu.VMEM((TICKS, NATIVE, HALF), F32),
+            pltpu.VMEM((TICKS, NATIVE, HALF), F32),
             pltpu.VMEM(tile, F32),
             pltpu.VMEM(tile, F32),
             pltpu.VMEM((TICKS,) + tile, F32),
@@ -399,16 +501,23 @@
             relay,
             relay,
             pltpu.VMEM((PARTS, NY - 1, NZ, PIECE, C), F32),
-            pltpu.VMEM((PARTS, NZ, PIECE, C), F32),
-            pltpu.VMEM((PARTS, NZ - 1, PIECE, C), F32),
+            pltpu.VMEM((PARTS, NZ // QUAD, QUAD, PIECE, C), F32),
+            pltpu.VMEM((PARTS, QUAD - 1, NZ // QUAD, PIECE, C), F32),
+            pltpu.VMEM((PARTS, NZ // QUAD, PIECE, C), F32),
+            pltpu.VMEM((PARTS, PIECE, C), F32),
             dma((TICKS - 1,)),
             dma((TICKS - 1,)),
             dma((TICKS - 1,)),
             dma((TICKS - 1,)),
             dma((PARTS, NY - 1)),
             dma((PARTS, NY - 1)),
-            dma((PARTS, NZ - 1)),
-            dma((PARTS, NZ - 1)),
+            dma((PARTS, QUAD - 1)),
+            dma((PARTS, QUAD - 1)),
+            dma((PARTS,)),
+            dma((PARTS,)),
+            dma((7,)),
+            dma((TICKS,)),
+            dma((TICKS,)),
         ],
         compiler_params=pltpu.CompilerParams(
             collective_id=0, has_side_effects=True, vmem_limit_bytes=60 * 1024 * 1024

time: 135 us -> 133 us (0.985)
  the two profiles are of different devices: /device:TPU:4 before, /device:TPU:454 now
where the time goes in v3:
time: 133 us
  Pallas kernels  127 us (95%)
  local copies, waits for them, and re-layouts  4.49 us (3%)
    pallas_call x1, Pallas kernels, shards(): pl.pallas_call(kernel, out_shape=(jax.ShapeDtypeStruct((TICKS, NATIVE, HA...  127 us
    unnamed x7, local copies, waits for them, and re-layouts  4.49 us

profile of v3, /device:TPU:454, one launch (start us, length us, event | category | flops | bytes accessed | tf_op | source)
XLA Modules:
  0.0 132.5 jit_solution(16482951590135631501)
XLA Ops:
  0.6 127.4 %shard_map.139 = (f32[4,576,128]{2,1,0:T(8,128)}, f32[4,576,128]{2,1,0:T(8,128)}, f32[72,256]{1,0:T(8,128)}) custom-call(s32[3]{0:T(128)} %order_ref.1, bf16[576,128]{1,0:T(8,128)(2,1)} %bitcast.45, bf16[3,576,128]{2,1,0:T(8,128)(2,1)} %bitcast.43, bf16[4,576,128]{2,1,0:T(8,128)(2,1)} %bitcast.42, bf16[576,128]{1,0:T(8,128)(2,1)} %bitcast.46, ...), custom_call_target="tpu_custom_call" | custom-call | tf_op jit(solution)/shard_map/pallas_call | solution.py:466
  128.0 0.0 copy-start
  128.0 2.8 %copy.25 = f32[4,1,2,12,12,256]{5,2,4,3,1,0:T(2,128)} copy(f32[4,1,2,12,12,256]{5,2,4,3,1,0:T(2,128)} %bitcast.41) | data formatting | bytes 2359296
  130.8 0.0 copy-done
  130.9 0.0 copy-start.1
  130.9 1.0 copy.26
  131.9 0.0 copy-done.1
  131.9 0.6 copy.27
Async XLA Ops:
  128.0 2.8 %copy-start = (f32[4,576,128]{2,1,0:T(8,128)S(1)}, f32[4,576,128]{2,1,0:T(8,128)}, u32[]{:S(2)}) copy-start(f32[4,576,128]{2,1,0:T(8,128)} %get-tuple-element.7) | copy-start | bytes 3538948
  130.9 1.0 copy-start.1

commit v4 on v3

--- a/solution.py
+++ b/solution.py
@@ -209,6 +209,11 @@
         def _():
             sender(*stream).start()
 
+    def send_from(core, *stream):
+        @pl.when(jnp.logical_and(section < SECTIONS - 1, lax.rem(section, 2) == core))
+        def _():
+            sender(*stream).start()
+
     def sent(*stream):
         @pl.when(section < SECTIONS - 1)
         def _():
@@ -300,37 +305,31 @@
     act_out[0] = forward()
     pl.semaphore_wait(barrier, 2 + NY - 1 + QUAD)
     send_on(*grad_stream(0))
+    send_from(0, *act_stream(0))
     store(returned_side, 0, grad_out[0])
+    store(emitted_side, 0, act_out[0])
+    prepare(1)
+    loads[5].wait()
+    loads[6].wait()
     turn(0)
     weight_terms(0)
-    for tick in range(1, TICKS):
-        prepare(tick)
-    turn(1)
-    turn(2)
-    turn(3)
-    sent(*grad_stream(0))
-    send_on(*act_stream(0))
-    store(emitted_side, 0, act_out[0])
-    loads[5].wait()
-    loads[6].wait()
 
     take(e_buf, fresh_grad_ref, grad_stream(0), 1)
     grad_out[1] = backward(1)
-    sent(*act_stream(0))
+    sent(*grad_stream(0))
     send_on(*grad_stream(1))
     store(returned_side, 1, grad_out[1])
+    turn(1)
     weight_terms(1)
-    take(x_buf, fresh_act_ref, act_stream(0), 1)
-    act_out[1] = forward()
-    store(emitted_side, 1, act_out[1])
-
+    for tick in (2, 3):
+        prepare(tick)
+        turn(tick)
     take(e_buf, fresh_grad_ref, grad_stream(1), 2)
     grad_out[2] = backward(2)
+    sent(*grad_stream(1))
     send_on(*grad_stream(2))
     store(returned_side, 2, grad_out[2])
     weight_terms(2)
-    sent(*grad_stream(2))
-    send_on(*act_stream(1))
 
     take(e_buf, fresh_grad_ref, grad_stream(2), 3)
     store(returned_side, 3, backward(3))
@@ -388,33 +387,39 @@
             y_copy(part, k).start()
 
     y_start(0)
+    sent(*grad_stream(2))
+    send_from(1, *act_stream(0))
+    take(x_buf, fresh_act_ref, act_stream(0), 1)
+    act_out[1] = forward()
+    send_from(0, *act_stream(1))
+    store(emitted_side, 1, act_out[1])
+    y_start(1)
+    y_done(0)
+    sent(*act_stream(0))
+    send_from(1, *act_stream(1))
+    y_start(2)
+    y_done(1)
     take(x_buf, fresh_act_ref, act_stream(1), 2)
     act_out[2] = forward()
     sent(*act_stream(1))
     send_on(*act_stream(2))
     store(emitted_side, 2, act_out[2])
-    for part in range(1, PARTS):
-        y_start(part)
-        y_done(part - 1)
-
-    take(x_buf, fresh_act_ref, act_stream(2), 3)
-    store(emitted_side, 3, forward())
-
-    y_done(PARTS - 1)
-
+    y_done(2)
     for part in range(PARTS):
         for k in range(1, QUAD):
             z_copy(part, k).wait_recv()
         z_mid[part] = y_sum[part, :, my_w] + (z_in[part, 0] + z_in[part, 1] + z_in[part, 2])
         far_copy(part).start()
 
+    take(x_buf, fresh_act_ref, act_stream(2), 3)
+    store(emitted_side, 3, forward())
+
     for part in range(PARTS):
         far_copy(part).wait_recv()
         block = z_mid[part, my_q] + far_in[part]
         wgrad_ref[part * PIECE : (part + 1) * PIECE] = block * (1.0 / BATCH)
 
-    for stream in (grad_stream(1), act_stream(2)):
-        sent(*stream)
+    sent(*act_stream(2))
 
     for k in range(1, NY):
         y_copy(PARTS - 1, k).wait_send()

time: 133 us -> 123 us (0.925)
  the two profiles are of different devices: /device:TPU:454 before, /device:TPU:294 now
where the time goes in v4:
time: 123 us
  Pallas kernels  118 us (96%)
  local copies, waits for them, and re-layouts  4.49 us (4%)
    pallas_call x1, Pallas kernels, shards(): pl.pallas_call(kernel, out_shape=(jax.ShapeDtypeStruct((TICKS, NATIVE, HA...  118 us
    unnamed x7, local copies, waits for them, and re-layouts  4.49 us

profile of v4, /device:TPU:294, one launch (start us, length us, event | category | flops | bytes accessed | tf_op | source)
XLA Modules:
  0.0 122.8 jit_solution(1279436637475067606)
XLA Ops:
  0.6 117.6 %shard_map.139 = (f32[4,576,128]{2,1,0:T(8,128)}, f32[4,576,128]{2,1,0:T(8,128)}, f32[72,256]{1,0:T(8,128)}) custom-call(s32[3]{0:T(128)} %order_ref.1, bf16[576,128]{1,0:T(8,128)(2,1)} %bitcast.45, bf16[3,576,128]{2,1,0:T(8,128)(2,1)} %bitcast.43, bf16[4,576,128]{2,1,0:T(8,128)(2,1)} %bitcast.42, bf16[576,128]{1,0:T(8,128)(2,1)} %bitcast.46, ...), custom_call_target="tpu_custom_call" | custom-call | tf_op jit(solution)/shard_map/pallas_call | solution.py:471
  118.3 0.0 copy-start
  118.3 2.8 %copy.25 = f32[4,1,2,12,12,256]{5,2,4,3,1,0:T(2,128)} copy(f32[4,1,2,12,12,256]{5,2,4,3,1,0:T(2,128)} %bitcast.41) | data formatting | bytes 2359296
  121.1 0.0 copy-done
  121.1 0.0 copy-start.1
  121.1 1.0 copy.26
  122.1 0.0 copy-done.1
  122.1 0.6 copy.27
Async XLA Ops:
  118.3 2.8 %copy-start = (f32[4,576,128]{2,1,0:T(8,128)S(1)}, f32[4,576,128]{2,1,0:T(8,128)}, u32[]{:S(2)}) copy-start(f32[4,576,128]{2,1,0:T(8,128)} %get-tuple-element.7) | copy-start | bytes 3538948
  121.1 1.0 copy-start.1

commit v5 on v4

--- a/solution.py
+++ b/solution.py
@@ -380,23 +380,26 @@
             z_copy(part, k).start()
 
     def y_start(part):
-        if part > 0:
-            for k in range(1, NY):
-                y_copy(part - 1, k).wait_send()
         for k in (2, 1, 3):
             y_copy(part, k).start()
 
+    def y_sent(part):
+        for k in range(1, NY):
+            y_copy(part, k).wait_send()
+
     y_start(0)
+    y_start(1)
     sent(*grad_stream(2))
     send_from(1, *act_stream(0))
     take(x_buf, fresh_act_ref, act_stream(0), 1)
     act_out[1] = forward()
     send_from(0, *act_stream(1))
     store(emitted_side, 1, act_out[1])
-    y_start(1)
+    y_sent(0)
     y_done(0)
     sent(*act_stream(0))
     send_from(1, *act_stream(1))
+    y_sent(1)
     y_start(2)
     y_done(1)
     take(x_buf, fresh_act_ref, act_stream(1), 2)
@@ -421,8 +424,7 @@
 
     sent(*act_stream(2))
 
-    for k in range(1, NY):
-        y_copy(PARTS - 1, k).wait_send()
+    y_sent(PARTS - 1)
     for part in range(PARTS):
         for k in range(1, QUAD):
             z_copy(part, k).wait_send()

time: 123 us -> 122 us (level)
  no operation moved by 1% of the time
where the time goes in v5:
time: 122 us
  Pallas kernels  117 us (96%)
  local copies, waits for them, and re-layouts  4.49 us (4%)
    pallas_call x1, Pallas kernels, shards(): pl.pallas_call(kernel, out_shape=(jax.ShapeDtypeStruct((TICKS, NATIVE, HA...  117 us
    unnamed x7, local copies, waits for them, and re-layouts  4.49 us

profile of v5, /device:TPU:294, one launch (start us, length us, event | category | flops | bytes accessed | tf_op | source)
XLA Modules:
  0.0 122.1 jit_solution(7941150521266167193)
XLA Ops:
  0.6 117.0 %shard_map.139 = (f32[4,576,128]{2,1,0:T(8,128)}, f32[4,576,128]{2,1,0:T(8,128)}, f32[72,256]{1,0:T(8,128)}) custom-call(s32[3]{0:T(128)} %order_ref.1, bf16[576,128]{1,0:T(8,128)(2,1)} %bitcast.45, bf16[3,576,128]{2,1,0:T(8,128)(2,1)} %bitcast.43, bf16[4,576,128]{2,1,0:T(8,128)(2,1)} %bitcast.42, bf16[576,128]{1,0:T(8,128)(2,1)} %bitcast.46, ...), custom_call_target="tpu_custom_call" | custom-call | tf_op jit(solution)/shard_map/pallas_call | solution.py:473
  117.6 0.0 copy-start
  117.6 2.8 %copy.25 = f32[4,1,2,12,12,256]{5,2,4,3,1,0:T(2,128)} copy(f32[4,1,2,12,12,256]{5,2,4,3,1,0:T(2,128)} %bitcast.41) | data formatting | bytes 2359296
  120.5 0.0 copy-done
  120.5 0.0 copy-start.1
  120.5 1.0 copy.26
  121.5 0.0 copy-done.1
  121.5 0.6 copy.27
Async XLA Ops:
  117.6 2.8 %copy-start = (f32[4,576,128]{2,1,0:T(8,128)S(1)}, f32[4,576,128]{2,1,0:T(8,128)}, u32[]{:S(2)}) copy-start(f32[4,576,128]{2,1,0:T(8,128)} %get-tuple-element.7) | copy-start | bytes 3538948
  120.5 1.0 copy-start.1
